TPU v7x, 32 devices: a whole 2x2x4 slice. The times are simulated.
32 devices in a mesh: frame: 4 (over y, x), head: 8 (over z, core).
Axes of the slice: x: 2, y: 2, z: 4, core: 2. Of those that a mesh axis runs over, the one named last changes fastest.
Arguments:
- tokens: bfloat16 [4096, 5120], P('frame', 'head'), may hold values from -16 to 16
- qkv_weight: bfloat16 [3, 5120, 2048], P(None, None, 'head'), may hold values from -0.1118034 to 0.1118034
- out_weight: bfloat16 [2048, 5120], P('head'), may hold values from -0.1875 to 0.1875
- modulation: float32 [3, 5120], replicated, may hold values from -3 to 3
- block_mask: int32 [16, 32, 32], P('head', 'frame'), may hold values from 0 to 1, as said below
Outputs:
- mixed: bfloat16 [4096, 5120], P('frame', 'head')
Inputs may be any that keep to these rules, and one draw needn't show every extreme that they name: `block_mask`: 1 keeps a pair of 128-token blocks; every query block keeps its own block.
All inputs are finite; a program needn't handle non-finite values.
Results may differ from a plain program's by a relative error of at most 0.0085.
Values may be sent and summed in bfloat16 or wider, within the bound.
A program may use at most 256 MiB of HBM per device.

v0:
```python
import functools
import math

import jax
import jax.numpy as jnp
from jax import lax
from jax.experimental import pallas as pl
from jax.experimental.pallas import tpu as pltpu
from jax.sharding import PartitionSpec as P

BLK = 128
NEGATIVE = -1e30
EPSILON = 1e-06
LOG2E = math.log2(math.e)
AHEAD = 4
LAG = 2
GROUP = 4
VMEM_BYTES = 52 * 2**20


def source_of(me, size, step):
    if size & (size - 1) == 0:
        return lax.bitwise_xor(me, step)
    return lax.rem(me + size - step, size)


def target_of(me, size, step):
    if size & (size - 1) == 0:
        return lax.bitwise_xor(me, step)
    return lax.rem(me + step, size)


def chain(me, size):
    return me // 2, me % 2, me + 1 - 2 * (me % 2)


def send(src, dst, send_sem, recv_sem, **where):
    return pltpu.make_async_remote_copy(
        src_ref=src,
        dst_ref=dst,
        send_sem=send_sem,
        recv_sem=recv_sem,
        device_id=where,
        device_id_type=pl.DeviceIdType.MESH,
    )


class Relay:
    def __init__(self, me, size, buffer, span, sems):
        self.me, self.size, self.buffer, self.span = me, size, buffer, span
        self.spot, self.core, self.other = chain(me, size)
        self.line = size // 2
        self.far_send, self.far_recv, self.pair_send, self.pair_recv = sems

    def rows(self, block, chunk):
        start = pl.multiple_of(chunk * self.span, self.span)
        return self.buffer.at[block, pl.ds(start, self.span), :]

    def hop(self, block, chunk, away, source=None):
        ref = self.rows(block, chunk)
        return send(
            ref if source is None else source,
            ref,
            self.far_send.at[0],
            self.far_recv.at[block // 2, chunk],
            head=self.me + 2 * away,
        )

    def pair(self, block, chunk, source=None):
        ref = self.rows(block, chunk)
        return send(
            ref if source is None else source,
            ref,
            self.pair_send.at[0],
            self.pair_recv.at[chunk],
            head=self.other,
        )

    def own(self, chunk, source=None):
        for away in (1, -1):
            edge = self.spot < self.line - 1 if away > 0 else self.spot > 0

            @pl.when(edge)
            def _():
                self.hop(self.me, chunk, away, source).start()

        self.pair(self.me, chunk, source).start()

    def pass_on(self, chunk, distance, ends=None):
        for away in (1, -1):
            spot = self.spot - away * distance
            here = spot >= 0 if away > 0 else spot < self.line
            edge = self.spot < self.line - 1 if away > 0 else self.spot > 0
            block = spot * 2 + self.core
            if ends is not None:
                far = 0 if away > 0 else self.line - 1
                here = spot == far if ends else jnp.logical_and(here, spot != far)

            @pl.when(here)
            def _():
                self.hop(block, chunk, away).wait_recv()

                @pl.when(edge)
                def _():
                    self.hop(block, chunk, away).start()

                self.pair(block, chunk).start()

    def advance(self, turn, count, ends=None):
        for distance in range(1, self.line):
            chunk = turn - (distance - 1)

            @pl.when(jnp.logical_and(chunk >= 0, chunk < count))
            def _():
                self.pass_on(chunk, distance, ends)

    def pass_all(self, chunk, ends):
        for distance in range(1, self.line):
            self.pass_on(chunk, distance, ends)

    def collect(self, chunk):
        start = pl.multiple_of(chunk * self.span, self.span)
        ref = self.buffer.at[pl.ds(0, self.line), pl.ds(start, self.span), :]
        send(
            ref, ref, self.pair_send.at[0], self.pair_recv.at[chunk], head=self.other
        ).wait_recv()

    def sent(self, blocks, sem):
        ref = self.buffer.at[pl.ds(0, blocks)]
        send(ref, ref, sem, self.pair_recv.at[0], head=self.other).wait_send()

    def drain(self):
        self.sent(self.line, self.pair_send.at[0])
        for spot in range(self.line):
            up = spot + 1 if spot < self.line - 1 else 0
            down = self.line - spot if spot > 0 else 0
            if up + down:

                @pl.when(self.spot == spot)
                def _():
                    self.sent(up + down, self.far_send.at[0])


def greet(me, frame, heads_axis, frames):
    barrier = pltpu.get_barrier_semaphore()
    for s in range(1, frames):
        pl.semaphore_signal(
            barrier, inc=1, device_id={"frame": target_of(frame, frames, s)},
            device_id_type=pl.DeviceIdType.MESH,
        )
    for s in range(1, heads_axis):
        pl.semaphore_signal(
            barrier, inc=1, device_id={"head": target_of(me, heads_axis, s)},
            device_id_type=pl.DeviceIdType.MESH,
        )
    pl.semaphore_wait(barrier, frames + heads_axis - 2)


def contract(parts, weight):
    cols = parts[0].shape[1]
    if cols % 128 == 0:
        return jnp.dot(
            jnp.concatenate(parts, axis=1), weight, preferred_element_type=jnp.float32
        )
    total = 0.0
    for i, part in enumerate(parts):
        total += jnp.dot(
            part, weight[i * cols : (i + 1) * cols], preferred_element_type=jnp.float32
        )
    return total


def block_kernel(
    frames, heads_axis, heads, count, group, w_slice, tokens, adjust, weight, out_weight, mask_in,
    gate_in, out_ref, got, held, q_ref, kv_ref, band_ref, full, done,
    peak, mass, blend, mixed, modulation, gate, mask_ref,
    t_far_send, t_far_recv, t_pair_send, t_pair_recv,
    h_far_send, h_far_recv, h_pair_send, h_pair_recv,
    kv_send, kv_recv, w_send, w_recv, x_send, x_recv, local, o_sem,
):
    me, frame = lax.axis_index("head"), lax.axis_index("frame")
    rows, cols = tokens.shape
    span = rows // count
    inner = q_ref.shape[1]
    width = cols * heads_axis
    line = heads_axis // 2
    share = band_ref.shape[1]
    head_size = inner // heads
    factor = LOG2E / math.sqrt(head_size)
    inside = jnp.logical_and(me // 2 > 0, me // 2 < line - 1)

    load = pltpu.make_async_copy(weight, held, local.at[0])
    load.start()
    mine = pltpu.make_async_copy(tokens, got.at[me], local.at[1])
    mine.start()
    tune = pltpu.make_async_copy(adjust, modulation, local.at[4])
    tune.start()
    hide = pltpu.make_async_copy(mask_in, mask_ref, local.at[6])
    hide.start()
    open_gate = pltpu.make_async_copy(gate_in, gate, local.at[5])
    open_gate.start()
    band = pl.ds(pl.multiple_of(frame * share, share), share)
    keep = pltpu.make_async_copy(w_slice(out_weight, band, me), band_ref.at[me], local.at[2])
    keep.start()
    greet(me, frame, heads_axis, frames)
    relay = Relay(me, heads_axis, got, span, (t_far_send, t_far_recv, t_pair_send, t_pair_recv))
    spread = Relay(me, heads_axis, done, span, (h_far_send, h_far_recv, h_pair_send, h_pair_recv))

    def rows_of(chunk):
        return pl.ds(pl.multiple_of(chunk * span, span), span)

    def begin(chunk, carry):
        relay.own(chunk, tokens.at[rows_of(chunk), :])
        return carry

    square = frames == 4

    def to_frame(chunk, s):
        window = rows_of(chunk)
        return send(
            kv_ref.at[0, :, window, :],
            kv_ref.at[s, :, window, :],
            kv_send.at[0],
            kv_recv.at[chunk, s - 1],
            frame=target_of(frame, frames, s),
        )

    def over(chunk, half):
        window = rows_of(chunk)
        near, there = (1, 2) if half == 0 else (2, 1)
        return send(
            kv_ref.at[near, half, window, :],
            kv_ref.at[3, half, window, :],
            kv_send.at[0],
            kv_recv.at[chunk, 2],
            frame=target_of(frame, frames, there),
        )

    def far_pair(chunk):
        ref = kv_ref.at[3, :, rows_of(chunk), :]
        return send(
            ref, ref, kv_send.at[0], kv_recv.at[chunk, 2], frame=target_of(frame, frames, 1)
        )

    direct = (1, 2) if square else tuple(range(1, frames))

    def relay_pair(chunk):
        for half in range(2 if square else 0):
            to_frame(chunk, half + 1).wait_recv()
            over(chunk, half).start()

    def heard(chunk):
        if square:
            far_pair(chunk).wait_recv()
        else:
            for s in direct:
                to_frame(chunk, s).wait_recv()

    def to_head(s):
        there = target_of(me, heads_axis, s)
        return send(
            w_slice(out_weight, band, there), band_ref.at[me], w_send.at[0], w_recv.at[0],
            head=there,
        )

    def bands():
        ref = band_ref.at[pl.ds(0, heads_axis - 1)]
        return send(
            ref, ref, w_send.at[0], w_recv.at[0], head=target_of(me, heads_axis, 1)
        )

    lay = pltpu.make_async_copy(band_ref, full.at[:, band, :], local.at[3])

    part = heads_axis // 2

    def slot_of(s, p):
        return p if square and s == p + 1 else 2

    def band_to(s, p):
        some = pl.ds(p * part, part)
        return send(
            band_ref.at[some], full.at[some, band, :], x_send.at[0], x_recv.at[slot_of(s, p)],
            frame=target_of(frame, frames, s),
        )

    def band_over(p):
        near, there = (1, 2) if p == 0 else (2, 1)
        part_rows = pl.ds(pl.multiple_of(source_of(frame, frames, near) * share, share), share)
        ref = full.at[pl.ds(p * part, part), part_rows, :]
        return send(
            ref, ref, x_send.at[0], x_recv.at[2], frame=target_of(frame, frames, there)
        )

    def band_near(p):
        ref = full.at[pl.ds(p * part, part), pl.ds(0, share), :]
        return send(
            ref, ref, x_send.at[0], x_recv.at[p], frame=target_of(frame, frames, p + 1)
        )

    def band_rest(count_of, slot):
        ref = full.at[:, pl.ds(0, count_of * share), :]
        return send(
            ref, ref, x_send.at[0], x_recv.at[slot], frame=target_of(frame, frames, 1)
        )

    late = jnp.maximum(jnp.maximum(me // 2, line - 1 - me // 2) - 1, 0)

    def give(later):
        for s in range(1, heads_axis):
            spot = target_of(me, heads_axis, s) // 2
            edge = jnp.logical_or(spot == 0, spot == line - 1)
            wait = jnp.logical_and(edge, spot != me // 2)

            @pl.when(wait if later else jnp.logical_not(wait))
            def _():
                to_head(s).start()

    def share_out(turn):
        for s in direct:
            band_to(s, (turn + s + 1) % 2).start()

    def pass_band():
        for p in range(2 if square else 0):
            band_near(p).wait_recv()
            band_over(p).start()

    def take():
        keep.wait()
        bands().wait_recv()
        lay.start()
        share_out(0)

    give(False)
    lax.fori_loop(0, jnp.where(inside, AHEAD, count), begin, 0)
    mine.wait()
    load.wait()
    tune.wait()
    hide.wait()
    open_gate.wait()

    def step(chunk):
        relay.collect(chunk)
        window = rows_of(chunk)
        total = jnp.zeros((span, cols), jnp.float32)
        for i in range(heads_axis):
            total += got[i, window, :].astype(jnp.float32)
        center = jnp.sum(total, axis=1, keepdims=True) / width
        square = jnp.zeros((span, cols), jnp.float32)
        for i in range(heads_axis):
            off = got[i, window, :].astype(jnp.float32) - center
            square += off * off
        inverse = lax.rsqrt(jnp.sum(square, axis=1, keepdims=True) / width + EPSILON)
        parts = []
        for i in range(heads_axis):
            wide_part = got[i, window, :].astype(jnp.float32)
            shift = modulation[0:1, i * cols : (i + 1) * cols]
            gain = modulation[1:2, i * cols : (i + 1) * cols]
            parts.append(
                ((wide_part - center) * inverse * (1.0 + gain) + shift).astype(jnp.bfloat16)
            )
        sums = [contract(parts, held[j]) for j in range(3)]
        q_ref[window, :] = sums[0].astype(q_ref.dtype)
        kv_ref[0, 0, window, :] = sums[1].astype(kv_ref.dtype)
        kv_ref[0, 1, window, :] = sums[2].astype(kv_ref.dtype)
        for s in direct:
            to_frame(chunk, s).start()

    sources = [source_of(frame, frames, s) * count for s in range(frames)]

    groups = count // group

    def fold(c):
        early = count - 1 - LAG
        key = jnp.where(c < count - 1, c - LAG, early)

        @pl.when(jnp.logical_and(key >= 0, c != count - 1))
        def _():
            heard(key)

        def each(g, carry):
            ready = (g + 1) * group - 1

            def one(k, carry):
                @pl.when(c == count - 1)
                def _():
                    for at, chunk in ((1, count - 2), (4, count - 1)):

                        @pl.when(k == min(at, early - 1))
                        def _():
                            relay_pair(chunk)

                    @pl.when(jnp.logical_and(k == early - 1, jnp.logical_not(inside)))
                    def _():
                        take()
                        share_out(1)

                @pl.when(jnp.logical_and(c == count, jnp.logical_and(g == 0, k > key)))
                def _():
                    heard(k)

                weigh(g * group, k)

                @pl.when(k == count - 1)
                def _():
                    for a in range(group):
                        settle(g * group + a)

                    @pl.when(jnp.logical_and(inside, g > 0))
                    def _():
                        for a in range(group):
                            spread.pass_all((g - 1) * group + a, False)

                return carry

            first = jnp.where(
                c < count - 1, jnp.where(c == ready, 0, jnp.maximum(key, 0)),
                jnp.where(c == count - 1, 0, key),
            )
            last = jnp.where(
                c < count - 1, jnp.where(c >= ready, key + 1, 0),
                jnp.where(c == count - 1, jnp.where(g == groups - 1, early, 0), count),
            )
            lax.fori_loop(first, last, one, 0)
            return carry

        lax.fori_loop(0, groups, each, 0)

    def weigh(base, block):
        keys = rows_of(block)
        chains = [(h, base + a) for a in range(group) for h in range(heads)]
        lanes = [slice(h * head_size, (h + 1) * head_size) for h in range(heads)]
        held_state = [(peak[h, q], mass[h, q], blend[h, q]) for h, q in chains]
        asked = [q_ref[rows_of(q), lanes[h]] for h, q in chains]
        parts, soft, result = {}, {}, {}

        def score(i):
            h, q = chains[i]
            pieces = []
            for slot in range(frames):
                scores = lax.dot_general(
                    kv_ref[slot, 0, keys, lanes[h]], asked[i], (((1,), (1,)), ((), ())),
                    preferred_element_type=jnp.float32,
                )
                kept = mask_ref[h, q, sources[slot] + block] > 0
                pieces.append(scores * factor + jnp.where(kept, 0.0, NEGATIVE))
            parts[i] = pieces

        def soften(i):
            top, total, _ = held_state[i]
            new_top = top
            for p in parts[i]:
                new_top = jnp.maximum(new_top, jnp.max(p, axis=0, keepdims=True))
            fade = jnp.exp2(top - new_top)
            total = total * fade
            weights = [jnp.exp2(p - new_top) for p in parts[i]]
            for w in weights:
                total += jnp.sum(w, axis=0, keepdims=True)
            joined = jnp.concatenate([w.astype(jnp.bfloat16) for w in weights], axis=0)
            soft[i] = (new_top, total, fade, joined)

        def gather(i):
            h, q = chains[i]
            new_top, total, fade, joined = soft[i]
            values = jnp.concatenate(
                [kv_ref[slot, 1, keys, lanes[h]] for slot in range(frames)], axis=0
            )
            result[i] = new_top, total, held_state[i][2] * fade + lax.dot_general(
                values, joined, (((0,), (0,)), ((), ())), preferred_element_type=jnp.float32
            )

        for i in range(len(chains) + 2):
            if i < len(chains):
                score(i)
            if 0 <= i - 1 < len(chains):
                soften(i - 1)
            if 0 <= i - 2:
                gather(i - 2)
        for i, (h, q) in enumerate(chains):
            peak[h, q], mass[h, q], blend[h, q] = result[i]

    def settle(t):
        window = rows_of(t)
        for h in range(heads):
            lanes = slice(h * head_size, (h + 1) * head_size)
            done[me, window, lanes] = (blend[h, t] / mass[h, t]).T.astype(done.dtype)
        spread.own(t)

    peak[...] = jnp.full(peak.shape, NEGATIVE, jnp.float32)
    mass[...] = jnp.zeros(mass.shape, jnp.float32)
    blend[...] = jnp.zeros(blend.shape, jnp.float32)

    def turn(i, carry):
        @pl.when(jnp.logical_and(inside, i + AHEAD < count))
        def _():
            begin(i + AHEAD, 0)

        @pl.when(jnp.logical_and(inside, i == 1))
        def _():
            take()

        @pl.when(jnp.logical_and(inside, i == count + late))
        def _():
            share_out(1)

        relay.advance(i, count)

        @pl.when(i == count + late - 1)
        def _():
            give(True)

        @pl.when(i > late)
        def _():
            fold(i - late - 1)

        @pl.when(jnp.logical_and(i >= late, i < count + late))
        def _():
            step(i - late)

        @pl.when(jnp.logical_and(i > late, i < count + late - 1))
        def _():
            relay_pair(i - late - 1)

        return carry

    lax.fori_loop(0, count + late + 2, turn, 0)

    pass_band()

    def near(t, carry):
        spread.pass_all(t, False)
        return carry

    lax.fori_loop(jnp.where(inside, count - group, 0), count, near, 0)
    lay.wait()

    def out(t):
        spread.collect(t)
        window = rows_of(t)
        plane = full[...].reshape(heads_axis * inner, full.shape[2])
        total = contract([done[i, window, :] for i in range(heads_axis)], plane)
        if gate.shape[1] == cols:
            own = gate[...]
        else:
            own = gate[2:3, pl.ds(pl.multiple_of(me * cols, cols), cols)]
        wide_part = got[me, window, :].astype(jnp.float32)
        mixed[window, :] = (wide_part + own * total).astype(mixed.dtype)
        store(t).start()

    def store(t):
        window = rows_of(t)
        return pltpu.make_async_copy(
            mixed.at[window, :], out_ref.at[window, :], o_sem.at[0]
        )

    behind = line - 1

    def last(i, carry):
        spread.advance(i, count, True)

        @pl.when(i == behind)
        def _():
            band_rest(2 if square else frames - 1, 2).wait_recv()

        @pl.when(i >= behind)
        def _():
            out(i - behind)

        return carry

    lax.fori_loop(0, count + behind, last, 0)

    relay.drain()
    spread.drain()
    pltpu.make_async_copy(mixed, out_ref, o_sem.at[0]).wait()
    ref = kv_ref.at[pl.ds(0, frames - 1)]
    send(
        ref, ref, kv_send.at[0], kv_recv.at[0, 0], frame=target_of(frame, frames, 1)
    ).wait_send()
    bands().wait_send()
    band_rest(frames - 1, 2).wait_send()


def sublayer(frames, heads_axis, heads, tokens, modulation, weight, out_weight, mask, gate):
    rows, cols = tokens.shape
    inner = weight.shape[2]
    count = rows // BLK
    group = math.gcd(count, GROUP)
    line = heads_axis // 2
    away = pl.BlockSpec(memory_space=pl.ANY)
    held = pl.BlockSpec(memory_space=pltpu.HBM)
    sem = pltpu.SemaphoreType.DMA
    if cols % 128 == 0:
        def w_slice(ref, band, there):
            return ref.at[band, pl.ds(pl.multiple_of(there * cols, cols), cols)]
    else:
        out_weight = out_weight.reshape(inner, heads_axis, cols).transpose(1, 0, 2)

        def w_slice(ref, band, there):
            return ref.at[there, band, :]

    relay_sems = [sem((1,)), sem((line, count)), sem((1,)), sem((count,))]
    return pl.pallas_call(
        functools.partial(block_kernel, frames, heads_axis, heads, count, group, w_slice),
        in_specs=[
            held, held, held, held, held, held,
        ],
        out_specs=away,
        out_shape=jax.ShapeDtypeStruct((rows, cols), jnp.bfloat16),
        scratch_shapes=[
            pltpu.VMEM((heads_axis, rows, cols), jnp.bfloat16),
            pltpu.VMEM(weight.shape, jnp.bfloat16),
            pltpu.VMEM((rows, inner), jnp.bfloat16),
            pltpu.VMEM((frames, 2, rows, inner), jnp.bfloat16),
            pltpu.VMEM((heads_axis, inner // frames, cols), jnp.bfloat16),
            pltpu.VMEM((heads_axis, inner, cols), jnp.bfloat16),
            pltpu.VMEM((heads_axis, rows, inner), jnp.bfloat16),
            pltpu.VMEM((heads, count, 1, BLK), jnp.float32),
            pltpu.VMEM((heads, count, 1, BLK), jnp.float32),
            pltpu.VMEM((heads, count, inner // heads, BLK), jnp.float32),
            pltpu.VMEM((rows, cols), jnp.bfloat16),
            pltpu.VMEM(modulation.shape, jnp.float32),
            pltpu.VMEM(gate.shape, jnp.float32),
            pltpu.SMEM(mask.shape, jnp.int32),
            *relay_sems,
            *relay_sems,
            sem((1,)),
            sem((count, frames - 1)),
            sem((1,)),
            sem((1,)),
            sem((1,)),
            sem((3,)),
            sem((7,)),
            sem((1,)),
        ],
        compiler_params=pltpu.CompilerParams(
            collective_id=0, has_side_effects=True, vmem_limit_bytes=VMEM_BYTES
        ),
        name="sublayer",
    )(*[
        pltpu.with_memory_space_constraint(x, pltpu.HBM)
        for x in (tokens, modulation, weight, out_weight, mask, gate)
    ])


def shards(frames, heads_axis, tokens, qkv_weight, out_weight, modulation, block_mask):
    local_cols = tokens.shape[1]
    gate = modulation
    if local_cols % 128:
        head = lax.axis_index("head")
        gate = lax.dynamic_slice_in_dim(modulation[2:3], head * local_cols, local_cols, 1)
    return sublayer(
        frames, heads_axis, block_mask.shape[0], tokens, modulation, qkv_weight, out_weight,
        block_mask, gate,
    )


def solution(mesh):
    placed = (
        P("frame", "head"),
        P(None, None, "head"),
        P("head", None),
        P(),
        P("head", "frame", None),
    )
    body = functools.partial(shards, mesh.shape["frame"], mesh.shape["head"])
    return jax.shard_map(
        body, mesh=mesh, in_specs=placed, out_specs=P("frame", "head"), check_vma=False
    )
```

profile of v0, /device:TPU:1, one launch (start us, length us, event | category | flops | bytes accessed | tf_op | source)
XLA Modules:
  0.0 140.7 jit_solution(13821158615281013597)
XLA Ops:
  0.0 139.7 %sublayer.1 = bf16[1024,640]{1,0:T(8,128)(2,1)S(1)} custom-call(bf16[1024,640]{1,0:T(8,128)(2,1)} %tokens.1, f32[3,5120]{1,0:T(4,128)} %gate_in.1, bf16[3,5120,256]{2,1,0:T(8,128)(2,1)} %weight.1, bf16[256,5120]{1,0:T(8,128)(2,1)} %out_weight.1, s32[2,8,32]{2,1,0:T(8,128)} %mask_in.1, f32[3,5120]{1,0:T(4,128)} %gate_in.1), custom_call_target="tpu_custom_call" | custom-call | tf_op jit(solution)/shard_map/sublayer/pallas_call | solution.py:602
  139.7 1.1 copy.7
where the time goes:
time: 141 us
  Pallas kernels  140 us (99%)
    pallas_call x1, Pallas kernels, sublayer(): pl.pallas_call(functools.partial(block_kernel, frames, heads_axis, heads,...  140 us

commit v1 on v0

--- a/solution.py
+++ b/solution.py
@@ -12,6 +12,7 @@
 NEGATIVE = -1e30
 EPSILON = 1e-06
 LOG2E = math.log2(math.e)
+FIRST = 2
 AHEAD = 4
 LAG = 2
 GROUP = 4
@@ -143,17 +144,48 @@
 
 def greet(me, frame, heads_axis, frames):
     barrier = pltpu.get_barrier_semaphore()
-    for s in range(1, frames):
+    spot, _, other = chain(me, heads_axis)
+    line = heads_axis // 2
+
+    def hail(**where):
         pl.semaphore_signal(
-            barrier, inc=1, device_id={"frame": target_of(frame, frames, s)},
-            device_id_type=pl.DeviceIdType.MESH,
-        )
-    for s in range(1, heads_axis):
-        pl.semaphore_signal(
-            barrier, inc=1, device_id={"head": target_of(me, heads_axis, s)},
-            device_id_type=pl.DeviceIdType.MESH,
-        )
-    pl.semaphore_wait(barrier, frames + heads_axis - 2)
+            barrier, inc=1, device_id=where, device_id_type=pl.DeviceIdType.MESH
+        )
+
+    near = (1, 2) if frames == 4 else range(1, frames)
+    for s in near:
+        hail(frame=target_of(frame, frames, s))
+    hail(head=other)
+
+    @pl.when(spot > 0)
+    def _():
+        hail(head=me - 2)
+
+    @pl.when(spot < line - 1)
+    def _():
+        hail(head=me + 2)
+
+    below = jnp.where(spot > 0, 1, 0)
+    above = jnp.where(spot < line - 1, 1, 0)
+    pl.semaphore_wait(barrier, len(near) + 1 + below + above)
+
+
+def roll_call(me, heads_axis, calls):
+    spot, _, _ = chain(me, heads_axis)
+    line = heads_axis // 2
+    for way, from_edge, to_edge in ((1, spot > 0, spot < line - 1), (-1, spot < line - 1, spot > 0)):
+        call = calls.at[0 if way > 0 else 1]
+
+        @pl.when(from_edge)
+        def _():
+            pl.semaphore_wait(call, 1)
+
+        @pl.when(to_edge)
+        def _():
+            pl.semaphore_signal(
+                call, inc=1, device_id={"head": me + 2 * way},
+                device_id_type=pl.DeviceIdType.MESH,
+            )
 
 
 def contract(parts, weight):
@@ -176,7 +208,7 @@
     peak, mass, blend, mixed, modulation, gate, mask_ref,
     t_far_send, t_far_recv, t_pair_send, t_pair_recv,
     h_far_send, h_far_recv, h_pair_send, h_pair_recv,
-    kv_send, kv_recv, w_send, w_recv, x_send, x_recv, local, o_sem,
+    kv_send, kv_recv, w_send, w_recv, x_send, x_recv, local, o_sem, calls,
 ):
     me, frame = lax.axis_index("head"), lax.axis_index("frame")
     rows, cols = tokens.shape
@@ -330,8 +362,10 @@
         lay.start()
         share_out(0)
 
+    lax.fori_loop(0, FIRST, begin, 0)
+    roll_call(me, heads_axis, calls)
     give(False)
-    lax.fori_loop(0, jnp.where(inside, AHEAD, count), begin, 0)
+    lax.fori_loop(FIRST, jnp.where(inside, AHEAD, count), begin, 0)
     mine.wait()
     load.wait()
     tune.wait()
@@ -533,9 +567,15 @@
     lax.fori_loop(jnp.where(inside, count - group, 0), count, near, 0)
     lay.wait()
 
+    both = math.gcd(count, 2)
+
+    def tall(t):
+        return pl.ds(pl.multiple_of(t * both * span, both * span), both * span)
+
     def out(t):
-        spread.collect(t)
-        window = rows_of(t)
+        for a in range(both):
+            spread.collect(t * both + a)
+        window = tall(t)
         plane = full[...].reshape(heads_axis * inner, full.shape[2])
         total = contract([done[i, window, :] for i in range(heads_axis)], plane)
         if gate.shape[1] == cols:
@@ -544,26 +584,20 @@
             own = gate[2:3, pl.ds(pl.multiple_of(me * cols, cols), cols)]
         wide_part = got[me, window, :].astype(jnp.float32)
         mixed[window, :] = (wide_part + own * total).astype(mixed.dtype)
-        store(t).start()
-
-    def store(t):
-        window = rows_of(t)
-        return pltpu.make_async_copy(
-            mixed.at[window, :], out_ref.at[window, :], o_sem.at[0]
-        )
+        pltpu.make_async_copy(mixed.at[window, :], out_ref.at[window, :], o_sem.at[0]).start()
 
     behind = line - 1
 
     def last(i, carry):
         spread.advance(i, count, True)
 
-        @pl.when(i == behind)
+        @pl.when(i == behind + both - 1)
         def _():
             band_rest(2 if square else frames - 1, 2).wait_recv()
 
-        @pl.when(i >= behind)
-        def _():
-            out(i - behind)
+        @pl.when(jnp.logical_and(i >= behind, (i - behind) % both == both - 1))
+        def _():
+            out((i - behind) // both)
 
         return carry
 
@@ -631,6 +665,7 @@
             sem((3,)),
             sem((7,)),
             sem((1,)),
+            pltpu.SemaphoreType.REGULAR((2,)),
         ],
         compiler_params=pltpu.CompilerParams(
             collective_id=0, has_side_effects=True, vmem_limit_bytes=VMEM_BYTES

time: 141 us -> 141 us (level)
  no operation moved by 1% of the time
where the time goes in v1:
time: 141 us
  Pallas kernels  139 us (99%)
    pallas_call x1, Pallas kernels, sublayer(): pl.pallas_call(functools.partial(block_kernel, frames, heads_axis, heads,...  139 us

profile of v1, /device:TPU:1, one launch (start us, length us, event | category | flops | bytes accessed | tf_op | source)
XLA Modules:
  0.0 140.5 jit_solution(7957206010811571479)
XLA Ops:
  0.0 139.4 %sublayer.1 = bf16[1024,640]{1,0:T(8,128)(2,1)S(1)} custom-call(bf16[1024,640]{1,0:T(8,128)(2,1)} %tokens.1, f32[3,5120]{1,0:T(4,128)} %gate_in.1, bf16[3,5120,256]{2,1,0:T(8,128)(2,1)} %weight.1, bf16[256,5120]{1,0:T(8,128)(2,1)} %out_weight.1, s32[2,8,32]{2,1,0:T(8,128)} %mask_in.1, f32[3,5120]{1,0:T(4,128)} %gate_in.1), custom_call_target="tpu_custom_call" | custom-call | tf_op jit(solution)/shard_map/sublayer/pallas_call | solution.py:636
  139.4 1.1 copy.7

commit v2 on v1

--- a/solution.py
+++ b/solution.py
@@ -13,7 +13,8 @@
 EPSILON = 1e-06
 LOG2E = math.log2(math.e)
 FIRST = 2
-AHEAD = 4
+OUTWARD = 6
+INWARD = 2
 LAG = 2
 GROUP = 4
 VMEM_BYTES = 52 * 2**20
@@ -77,15 +78,19 @@
             head=self.other,
         )
 
-    def own(self, chunk, source=None):
+    def own(self, chunk, source=None, outward=None):
+        low = self.spot < self.line // 2
         for away in (1, -1):
             edge = self.spot < self.line - 1 if away > 0 else self.spot > 0
+            if outward is not None:
+                edge = jnp.logical_and(edge, low == ((away < 0) == outward))
 
             @pl.when(edge)
             def _():
                 self.hop(self.me, chunk, away, source).start()
 
-        self.pair(self.me, chunk, source).start()
+        if outward is not False:
+            self.pair(self.me, chunk, source).start()
 
     def pass_on(self, chunk, distance, ends=None):
         for away in (1, -1):
@@ -241,9 +246,15 @@
     def rows_of(chunk):
         return pl.ds(pl.multiple_of(chunk * span, span), span)
 
-    def begin(chunk, carry):
-        relay.own(chunk, tokens.at[rows_of(chunk), :])
-        return carry
+    def begin(outward, chunk):
+        relay.own(chunk, tokens.at[rows_of(chunk), :], outward)
+
+    def launch(first, last, outward):
+        def one(chunk, carry):
+            begin(outward, chunk)
+            return carry
+
+        lax.fori_loop(first, last, one, 0)
 
     square = frames == 4
 
@@ -362,10 +373,12 @@
         lay.start()
         share_out(0)
 
-    lax.fori_loop(0, FIRST, begin, 0)
+    launch(0, FIRST, True)
+    launch(0, FIRST, False)
     roll_call(me, heads_axis, calls)
     give(False)
-    lax.fori_loop(FIRST, jnp.where(inside, AHEAD, count), begin, 0)
+    launch(FIRST, jnp.where(inside, OUTWARD, count), True)
+    launch(FIRST, jnp.where(inside, INWARD, count), False)
     mine.wait()
     load.wait()
     tune.wait()
@@ -524,9 +537,11 @@
     blend[...] = jnp.zeros(blend.shape, jnp.float32)
 
     def turn(i, carry):
-        @pl.when(jnp.logical_and(inside, i + AHEAD < count))
-        def _():
-            begin(i + AHEAD, 0)
+        for outward, ahead in ((True, OUTWARD), (False, INWARD)):
+
+            @pl.when(jnp.logical_and(inside, i + ahead < count))
+            def _():
+                begin(outward, i + ahead)
 
         @pl.when(jnp.logical_and(inside, i == 1))
         def _():

time: 141 us -> 139 us (0.986)
  Pallas kernels: 139 us -> 137 us
    pallas_call x1, Pallas kernels: 139 us -> 137 us  [sublayer(): pl.pallas_call(functools.partial(block_kernel, frames, heads_axis, heads,...]
where the time goes in v2:
time: 139 us; the launch traced here: 138 us
  Pallas kernels  137 us (99%)
    pallas_call x1, Pallas kernels, sublayer(): pl.pallas_call(functools.partial(block_kernel, frames, heads_axis, heads,...  137 us

profile of v2, /device:TPU:1, one launch (start us, length us, event | category | flops | bytes accessed | tf_op | source)
XLA Modules:
  0.0 138.2 jit_solution(9583017436845821867)
XLA Ops:
  0.0 137.2 %sublayer.1 = bf16[1024,640]{1,0:T(8,128)(2,1)S(1)} custom-call(bf16[1024,640]{1,0:T(8,128)(2,1)} %tokens.1, f32[3,5120]{1,0:T(4,128)} %gate_in.1, bf16[3,5120,256]{2,1,0:T(8,128)(2,1)} %weight.1, bf16[256,5120]{1,0:T(8,128)(2,1)} %out_weight.1, s32[2,8,32]{2,1,0:T(8,128)} %mask_in.1, f32[3,5120]{1,0:T(4,128)} %gate_in.1), custom_call_target="tpu_custom_call" | custom-call | tf_op jit(solution)/shard_map/sublayer/pallas_call | solution.py:651
  137.2 1.1 copy.7

commit v3 on v2

--- a/solution.py
+++ b/solution.py
@@ -582,7 +582,7 @@
     lax.fori_loop(jnp.where(inside, count - group, 0), count, near, 0)
     lay.wait()
 
-    both = math.gcd(count, 2)
+    both = 1
 
     def tall(t):
         return pl.ds(pl.multiple_of(t * both * span, both * span), both * span)

time: 139 us -> 138 us (level)
  no operation moved by 1% of the time
where the time goes in v3:
time: 138 us
  Pallas kernels  137 us (99%)
    pallas_call x1, Pallas kernels, sublayer(): pl.pallas_call(functools.partial(block_kernel, frames, heads_axis, heads,...  137 us

profile of v3, /device:TPU:1, one launch (start us, length us, event | category | flops | bytes accessed | tf_op | source)
XLA Modules:
  0.0 137.8 jit_solution(15576554284567536446)
XLA Ops:
  0.0 136.8 %sublayer.1 = bf16[1024,640]{1,0:T(8,128)(2,1)S(1)} custom-call(bf16[1024,640]{1,0:T(8,128)(2,1)} %tokens.1, f32[3,5120]{1,0:T(4,128)} %gate_in.1, bf16[3,5120,256]{2,1,0:T(8,128)(2,1)} %weight.1, bf16[256,5120]{1,0:T(8,128)(2,1)} %out_weight.1, s32[2,8,32]{2,1,0:T(8,128)} %mask_in.1, f32[3,5120]{1,0:T(4,128)} %gate_in.1), custom_call_target="tpu_custom_call" | custom-call | tf_op jit(solution)/shard_map/sublayer/pallas_call | solution.py:651
  136.8 1.1 copy.7
